TPU v7x, 512 devices: a whole 4x8x8 slice. The times are simulated.
512 devices in a mesh: dp: 4 (over x), ctx: 128 (over y, z, core).
Axes of the slice: x: 4, y: 8, z: 8, core: 2. Of those that a mesh axis runs over, the one named last changes fastest.
Arguments:
- tokens: bfloat16 [4, 32768, 4096], P('dp', 'ctx'), may hold values from -6 to 6
- queries: bfloat16 [4, 32768, 2048], P('dp', 'ctx'), may hold values from -260 to 260, as said below
- kv_weight: bfloat16 [4096, 1024], P('ctx', 'dp'), may hold values from -0.09375 to 0.09375
- doc_blocks: int32 [4, 64], P('dp'), may hold values from 1 to 8, 256 in all within a row
- block_mask: int32 [4, 256, 7], P('dp'), may hold values 0 or 1
- plan: int32 [4, 256], P('dp'), may hold values from 0 to 255, as said below
Outputs:
- attended: bfloat16 [4, 32768, 2048], P('dp', 'ctx')
- stats: float32 [4, 16, 32768], P('dp', None, 'ctx')
Inputs may be any that keep to these rules, and one draw needn't show every extreme that they name: queries of unit order, in some draws with a few rows far larger. `doc_blocks`: the documents of a pack in order, their lengths summing to 256. `block_mask`: entry [b, w] lets block b attend block b - w - 1 where that block is of the same document. plan[b] = ctx index * 2 + place; the slot lies on block b's own ctx index or on the one that differs from it in the lowest bit, and every slot is named by exactly one block.
All inputs are finite; a program needn't handle non-finite values.
Results may differ from a plain program's by a relative error of at most 0.012.
The roundings to bfloat16 on the way count: a program that leaves them out, or rounds other values in their place, can miss the bound.
Values may be sent and summed in bfloat16 or wider, within the bound.
A program may use at most 128 MiB of HBM per device.

v0:
```python
import math

import jax
import jax.numpy as jnp
from jax import lax
from jax.sharding import PartitionSpec as P

HD = 128
QH = 16
KVH = 4
BLK = 128
MAXDOC = 8


def from_partner(block, axis, stride):
    count = lax.axis_size(axis)
    route = []
    for low in range(count):
        high = low | 1 << stride
        if high != low and high < count:
            route += [(low, high), (high, low)]
    return lax.ppermute(block, axis, route)


def passed_along(array, axis, by):
    size = lax.axis_size(axis)
    pairs = [(i, i + by) for i in range(size) if 0 <= i + by < size]
    return lax.ppermute(array, axis, pairs)


def document_of_blocks(doc_blocks, count):
    ends = jnp.cumsum(doc_blocks)
    blocks = jnp.arange(count, dtype=jnp.int32)
    return jnp.sum((blocks[:, None] >= ends[None, :]).astype(jnp.int32), axis=1)


def attend_block(query_block, query_index, buffer, base, documents, mask_rows):
    count = documents.shape[0]
    group = QH // KVH
    slots = buffer.shape[0]
    scale = 1.0 / math.sqrt(HD)
    heads = query_block.reshape(BLK, KVH, group, HD)
    gate_row = lax.dynamic_index_in_dim(mask_rows, query_index, 0, keepdims=False)
    gates = jnp.concatenate([gate_row[::-1], jnp.ones((1,), jnp.int32)])
    key_index = query_index - (MAXDOC - 1) + jnp.arange(MAXDOC, dtype=jnp.int32)
    key_docs = jnp.where(key_index >= 0, documents[jnp.clip(key_index, 0, count - 1)], -1)
    allowed = (key_docs == documents[query_index]) & (gates == 1)
    places = jnp.arange(BLK, dtype=jnp.int32)
    causal = places[None, :] <= places[:, None]

    def fetch(step):
        local = jnp.clip(key_index[step] - base, 0, slots - 1)
        return lax.dynamic_index_in_dim(buffer, local, 0, keepdims=False)

    def find_scores(step, carry):

        def compute(state):
            table, running = state
            keys = fetch(step)[:, : KVH * HD].reshape(BLK, KVH, HD)
            scores = (
                jnp.einsum("ikgd,lkd->kgil", heads, keys, preferred_element_type=jnp.float32)
                * scale
            )
            keep = jnp.logical_or(step < MAXDOC - 1, causal)
            scores = jnp.where(keep[None, None], scores, -jnp.inf)
            table = lax.dynamic_update_index_in_dim(table, scores, step, 0)
            return (table, jnp.maximum(running, jnp.max(scores, axis=-1)))

        return lax.cond(allowed[step], compute, lambda state: state, carry)

    table = jnp.full((MAXDOC, KVH, group, BLK, BLK), -jnp.inf, jnp.float32)
    running = jnp.full((KVH, group, BLK), -jnp.inf, jnp.float32)
    table, rowmax = lax.fori_loop(0, MAXDOC, find_scores, (table, running))

    def accumulate(step, carry):

        def add(state):
            total, summed = state
            values = fetch(step)[:, KVH * HD :].reshape(BLK, KVH, HD)
            scores = lax.dynamic_index_in_dim(table, step, 0, keepdims=False)
            weights = jnp.exp(scores - rowmax[..., None])
            total = total + jnp.sum(weights, axis=-1)
            summed = summed + jnp.einsum(
                "kgil,lkd->kgid",
                weights.astype(jnp.bfloat16),
                values,
                preferred_element_type=jnp.float32,
            )
            return (total, summed)

        return lax.cond(allowed[step], add, lambda state: state, carry)

    start = (
        jnp.zeros((KVH, group, BLK), jnp.float32),
        jnp.zeros((KVH, group, BLK, HD), jnp.float32),
    )
    total, summed = lax.fori_loop(0, MAXDOC, accumulate, start)
    out = (
        (summed / total[..., None]).transpose(2, 0, 1, 3).reshape(BLK, QH * HD).astype(jnp.bfloat16)
    )
    stats = (rowmax + jnp.log(total)).reshape(QH, BLK)
    return (out, stats)


def body(tokens, queries, kv_weight, doc_blocks, block_mask, plan):
    local_tokens = tokens[0]
    columns = lax.all_gather(kv_weight, "dp", axis=1, tiled=True)
    projected = jnp.dot(
        local_tokens,
        lax.all_gather(columns, "ctx", axis=0, tiled=True),
        preferred_element_type=jnp.float32,
    ).astype(jnp.bfloat16)
    blocks_dev = local_tokens.shape[0] // BLK
    width = projected.shape[1]
    own_pairs = projected.reshape(blocks_dev, BLK, width)
    count = plan.shape[1]
    documents = document_of_blocks(doc_blocks[0], count)
    mask_rows = block_mask[0]
    plan_row = plan[0]
    device = lax.axis_index("ctx")
    first = device * blocks_dev
    local_ids = first + jnp.arange(blocks_dev, dtype=jnp.int32)
    every_block = jnp.arange(count, dtype=jnp.int32)
    sources = jnp.sum(
        jnp.where(plan_row[None, :] == local_ids[:, None], every_block[None, :], 0), axis=1
    )
    source_picks = jnp.where(sources // blocks_dev == device, 0, blocks_dev) + sources % blocks_dev
    own_queries = queries[0].reshape(blocks_dev, BLK, queries.shape[2])
    reach = (MAXDOC + blocks_dev - 2) // blocks_dev
    partner_queries = from_partner(own_queries, "ctx", 0)
    partner_pairs = from_partner(own_pairs, "ctx", 0)
    odd = device % 2
    pair_kv = jnp.where(
        odd == 0,
        jnp.concatenate([own_pairs, partner_pairs], axis=0),
        jnp.concatenate([partner_pairs, own_pairs], axis=0),
    )
    pair_reach = (reach + 1) // 2
    behind = [passed_along(pair_kv, "ctx", 2 * step) for step in range(pair_reach, 0, -1)]
    buffer = jnp.concatenate(behind + [pair_kv], axis=0)
    base = (device - odd - 2 * pair_reach) * blocks_dev
    candidates = jnp.concatenate([own_queries, partner_queries], axis=0)
    chosen = jnp.take(candidates, source_picks, axis=0)

    def run_planned(item):
        return attend_block(item[0], item[1], buffer, base, documents, mask_rows)

    planned_out, stats_blocks = lax.map(run_planned, (chosen, sources))
    partner_out = from_partner(planned_out, "ctx", 0)
    targets = lax.dynamic_slice_in_dim(plan_row, first, blocks_dev, 0)
    target_picks = jnp.where(targets // blocks_dev == device, 0, blocks_dev) + targets % blocks_dev
    returned = jnp.concatenate([planned_out, partner_out], axis=0)
    attended = jnp.take(returned, target_picks, axis=0)
    attended = attended.reshape(1, blocks_dev * BLK, attended.shape[2])
    stats = stats_blocks.transpose(1, 0, 2).reshape(1, QH, blocks_dev * BLK)
    return (attended, stats)


def solution(mesh):
    in_specs = (
        P("dp", "ctx", None),
        P("dp", "ctx", None),
        P("ctx", "dp"),
        P("dp", None),
        P("dp", None, None),
        P("dp", None),
    )
    out_specs = (P("dp", "ctx", None), P("dp", None, "ctx"))
    return jax.shard_map(body, mesh=mesh, in_specs=in_specs, out_specs=out_specs, check_vma=False)
```

profile of v0, /device:TPU:51, one launch (start us, length us, event | category | flops | bytes accessed | tf_op | source)
XLA Modules:
  0.0 450.6 jit_solution(10301877877669656119)
XLA Ops:
  7.2 10.1 %all_gather.6 = bf16[32,1024]{1,0:T(8,128)(2,1)} all-gather(bf16[32,256]{1,0:T(8,128)(2,1)} %param.20), channel_id=1, replica_groups=mesh['dp'=4,'ctx'=128] {'dp'}, dimensions={1}, use_global_device_ids=true | all-gather | bytes 81920 | tf_op jit(solution)/shard_map/all_gather | solution.py:107
  17.4 93.9 %all-gather.2.cloned.1.call-done = bf16[4096,1024]{1,0:T(8,128)(2,1)} async-done(((bf16[32,1024]{1,0:T(8,128)(2,1)}), bf16[4096,1024]{1,0:T(8,128)(2,1)}) %all-gather.2.cloned.1.call-update) | async-done | bytes 8388624 | tf_op jit(solution)/shard_map/all_gather | solution.py:110
  111.3 5.7 %fusion.19 = bf16[256,1024]{1,0:T(8,128)(2,1)S(1)} fusion(bf16[4096,1024]{1,0:T(8,128)(2,1)} %all-gather.2.cloned.1.call-done, bf16[1,256,4096]{2,1,0:T(8,128)(2,1)S(1)} %copy-done), kind=kOutput, calls=%fused_computation.40 | convolution fusion | flops 2147745792 | bytes 11010048 | tf_op jit(solution)/shard_map/dot_general | solution.py:108
  137.7 34.0 %collective-permute-done.2 = bf16[4,128,1024]{1,2,0:T(8,128)(2,1)} collective-permute-done((bf16[4,128,1024]{1,2,0:T(8,128)(2,1)}, bf16[4,128,1024]{1,2,0:T(8,128)(2,1)}, u32[]{:S(2)}, u32[]{:S(2)}) %collective-permute-start.2) | collective-permute-done | bytes 1048608 | tf_op jit(solution)/shard_map/ppermute | solution.py:28
  171.8 25.5 %collective-permute-done.3 = bf16[4,128,1024]{1,2,0:T(8,128)(2,1)} collective-permute-done((bf16[4,128,1024]{1,2,0:T(8,128)(2,1)}, bf16[4,128,1024]{1,2,0:T(8,128)(2,1)}, u32[]{:S(2)}, u32[]{:S(2)}) %collective-permute-start.3) | collective-permute-done | bytes 1048608 | tf_op jit(solution)/shard_map/ppermute | solution.py:28
  200.5 199.1 %while.68 = (s32[]{:T(128)}, bf16[2,128,2048]{2,1,0:T(8,128)(2,1)}, f32[2,16,128]{2,1,0:T(8,128)}, s32[2]{0:T(128)}, s32[256]{0:T(256)S(1)}, /*index=5*/s32[256,...) while((s32[]{:T(128)}, bf16[2,128,2048]{2,1,0:T(8,128)(2,1)}, ...), condition=%wide.region_14.16_spmd, body=%wide.region_3.15_spmd.sunk | while | flops 136875136 | bytes 44357780 | solution.py:148
  213.4 43.0 %while.69 = (s32[]{:T(128)}, f32[8,4,4,128,128]{3,4,2,1,0:T(8,128)}, f32[4,4,128]{2,1,0:T(4,128)S(1)}, pred[8]{0:T(512)(128)(4,1)S(1)}, s32[]{:T(128)}, /*index=...) while((s32[]{:T(128)}, ...), condition=%wide.region_8.9_spmd.clone, body=%wide.region_4.8_spmd.clone.sunk | while | flops 67928080 | bytes 4915628 | solution.py:73
  233.7 4.8 %conditional.6 = ((f32[8,4,4,128,128]{3,4,2,1,0:T(8,128)}, f32[4,4,128]{2,1,0:T(4,128)S(1)})) conditional(s32[]{:T(128)} %bitcast.102, (f32[8,4,4,128,128]{3,4,2,1,0:T(8,128)}, f32[4,4,128]{2,1,0:T(4,128)S(1)}) %tuple.130, (s32[]{:T(128)}, s32[128,128]{0,1:T(8,128)S(1)}, s32[]{:T(128)}, s32[]{:T(128)}, bf16[12,128,1024]{1,2,0:T(8,128)(2,1)}, ...), branch_computations={%region_5.5_spmd, %region_6.7_spmd} | conditional | flops 67928080 | bytes 4784324 | solution.py:69
  256.4 9.2 %copy.61 = f32[8,4,4,128,128]{4,3,2,1,0:T(8,128)} copy(f32[8,4,4,128,128]{3,4,2,1,0:T(8,128)} %get-tuple-element.890) | data formatting | bytes 16777216 | tf_op jit(solution)/shard_map/while
  265.7 54.0 %while.70 = (s32[]{:T(128)}, f32[4,4,128]{2,1,0:T(4,128)S(1)}, f32[4,4,128,128]{3,2,1,0:T(8,128)S(1)}, pred[8]{0:T(512)(128)(4,1)S(1)}, f32[8,4,4,128,128]{4,3,2...) while((s32[]{:T(128)}, f32[4,4,128]{2,1,0:T(4,128)S(1)}, ...), condition=%wide.region_13.14_spmd.clone, body=%wide.region_9.13_spmd.clone.sunk | while | flops 68419600 | bytes 5161378 | solution.py:97
  268.5 6.1 %conditional.7 = ((f32[4,4,128]{2,1,0:T(4,128)S(1)}, f32[4,4,128,128]{3,2,1,0:T(8,128)S(1)})) conditional(s32[]{:T(128)} %bitcast.103, (f32[4,4,128]{2,1,0:T(4,128)S(1)}, f32[4,4,128,128]{3,2,1,0:T(8,128)S(1)}) %tuple.133, (s32[]{:T(128)}, f32[8,4,4,128,128]{4,3,2,1,0:T(8,128)}, f32[4,4,128]{2,1,0:T(4,128)S(1)}, f32[4,4,128]{2,1,0:T(4,128)S(1)}, ...), branch_computations={%region_10.10_spmd, %region_11.12_spmd} | conditional | flops 68419600 | bytes 5161146 | solution.py:91
  276.0 6.1 %conditional.7 = ((f32[4,4,128]{2,1,0:T(4,128)S(1)}, f32[4,4,128,128]{3,2,1,0:T(8,128)S(1)})) conditional(s32[]{:T(128)} %bitcast.103, (f32[4,4,128]{2,1,0:T(4,128)S(1)}, f32[4,4,128,128]{3,2,1,0:T(8,128)S(1)}) %tuple.133, (s32[]{:T(128)}, f32[8,4,4,128,128]{4,3,2,1,0:T(8,128)}, f32[4,4,128]{2,1,0:T(4,128)S(1)}, f32[4,4,128]{2,1,0:T(4,128)S(1)}, ...), branch_computations={%region_10.10_spmd, %region_11.12_spmd} | conditional | flops 68419600 | bytes 5161146 | solution.py:91
  283.5 6.1 %conditional.7 = ((f32[4,4,128]{2,1,0:T(4,128)S(1)}, f32[4,4,128,128]{3,2,1,0:T(8,128)S(1)})) conditional(s32[]{:T(128)} %bitcast.103, (f32[4,4,128]{2,1,0:T(4,128)S(1)}, f32[4,4,128,128]{3,2,1,0:T(8,128)S(1)}) %tuple.133, (s32[]{:T(128)}, f32[8,4,4,128,128]{4,3,2,1,0:T(8,128)}, f32[4,4,128]{2,1,0:T(4,128)S(1)}, f32[4,4,128]{2,1,0:T(4,128)S(1)}, ...), branch_computations={%region_10.10_spmd, %region_11.12_spmd} | conditional | flops 68419600 | bytes 5161146 | solution.py:91
  291.0 6.1 %conditional.7 = ((f32[4,4,128]{2,1,0:T(4,128)S(1)}, f32[4,4,128,128]{3,2,1,0:T(8,128)S(1)})) conditional(s32[]{:T(128)} %bitcast.103, (f32[4,4,128]{2,1,0:T(4,128)S(1)}, f32[4,4,128,128]{3,2,1,0:T(8,128)S(1)}) %tuple.133, (s32[]{:T(128)}, f32[8,4,4,128,128]{4,3,2,1,0:T(8,128)}, f32[4,4,128]{2,1,0:T(4,128)S(1)}, f32[4,4,128]{2,1,0:T(4,128)S(1)}, ...), branch_computations={%region_10.10_spmd, %region_11.12_spmd} | conditional | flops 68419600 | bytes 5161146 | solution.py:91
  298.5 6.1 %conditional.7 = ((f32[4,4,128]{2,1,0:T(4,128)S(1)}, f32[4,4,128,128]{3,2,1,0:T(8,128)S(1)})) conditional(s32[]{:T(128)} %bitcast.103, (f32[4,4,128]{2,1,0:T(4,128)S(1)}, f32[4,4,128,128]{3,2,1,0:T(8,128)S(1)}) %tuple.133, (s32[]{:T(128)}, f32[8,4,4,128,128]{4,3,2,1,0:T(8,128)}, f32[4,4,128]{2,1,0:T(4,128)S(1)}, f32[4,4,128]{2,1,0:T(4,128)S(1)}, ...), branch_computations={%region_10.10_spmd, %region_11.12_spmd} | conditional | flops 68419600 | bytes 5161146 | solution.py:91
  306.0 6.1 %conditional.7 = ((f32[4,4,128]{2,1,0:T(4,128)S(1)}, f32[4,4,128,128]{3,2,1,0:T(8,128)S(1)})) conditional(s32[]{:T(128)} %bitcast.103, (f32[4,4,128]{2,1,0:T(4,128)S(1)}, f32[4,4,128,128]{3,2,1,0:T(8,128)S(1)}) %tuple.133, (s32[]{:T(128)}, f32[8,4,4,128,128]{4,3,2,1,0:T(8,128)}, f32[4,4,128]{2,1,0:T(4,128)S(1)}, f32[4,4,128]{2,1,0:T(4,128)S(1)}, ...), branch_computations={%region_10.10_spmd, %region_11.12_spmd} | conditional | flops 68419600 | bytes 5161146 | solution.py:91
  313.5 6.1 %conditional.7 = ((f32[4,4,128]{2,1,0:T(4,128)S(1)}, f32[4,4,128,128]{3,2,1,0:T(8,128)S(1)})) conditional(s32[]{:T(128)} %bitcast.103, (f32[4,4,128]{2,1,0:T(4,128)S(1)}, f32[4,4,128,128]{3,2,1,0:T(8,128)S(1)}) %tuple.133, (s32[]{:T(128)}, f32[8,4,4,128,128]{4,3,2,1,0:T(8,128)}, f32[4,4,128]{2,1,0:T(4,128)S(1)}, f32[4,4,128]{2,1,0:T(4,128)S(1)}, ...), branch_computations={%region_10.10_spmd, %region_11.12_spmd} | conditional | flops 68419600 | bytes 5161146 | solution.py:91
  334.6 24.2 %while.69 = (s32[]{:T(128)}, f32[8,4,4,128,128]{3,4,2,1,0:T(8,128)}, f32[4,4,128]{2,1,0:T(4,128)S(1)}, pred[8]{0:T(512)(128)(4,1)S(1)}, s32[]{:T(128)}, /*index=...) while((s32[]{:T(128)}, ...), condition=%wide.region_8.9_spmd.clone, body=%wide.region_4.8_spmd.clone.sunk | while | flops 67928080 | bytes 4915628 | solution.py:73
  358.7 9.2 %copy.61 = f32[8,4,4,128,128]{4,3,2,1,0:T(8,128)} copy(f32[8,4,4,128,128]{3,4,2,1,0:T(8,128)} %get-tuple-element.890) | data formatting | bytes 16777216 | tf_op jit(solution)/shard_map/while
  368.1 29.5 %while.70 = (s32[]{:T(128)}, f32[4,4,128]{2,1,0:T(4,128)S(1)}, f32[4,4,128,128]{3,2,1,0:T(8,128)S(1)}, pred[8]{0:T(512)(128)(4,1)S(1)}, f32[8,4,4,128,128]{4,3,2...) while((s32[]{:T(128)}, f32[4,4,128]{2,1,0:T(4,128)S(1)}, ...), condition=%wide.region_13.14_spmd.clone, body=%wide.region_9.13_spmd.clone.sunk | while | flops 68419600 | bytes 5161378 | solution.py:97
  376.4 6.1 %conditional.7 = ((f32[4,4,128]{2,1,0:T(4,128)S(1)}, f32[4,4,128,128]{3,2,1,0:T(8,128)S(1)})) conditional(s32[]{:T(128)} %bitcast.103, (f32[4,4,128]{2,1,0:T(4,128)S(1)}, f32[4,4,128,128]{3,2,1,0:T(8,128)S(1)}) %tuple.133, (s32[]{:T(128)}, f32[8,4,4,128,128]{4,3,2,1,0:T(8,128)}, f32[4,4,128]{2,1,0:T(4,128)S(1)}, f32[4,4,128]{2,1,0:T(4,128)S(1)}, ...), branch_computations={%region_10.10_spmd, %region_11.12_spmd} | conditional | flops 68419600 | bytes 5161146 | solution.py:91
  383.9 6.1 %conditional.7 = ((f32[4,4,128]{2,1,0:T(4,128)S(1)}, f32[4,4,128,128]{3,2,1,0:T(8,128)S(1)})) conditional(s32[]{:T(128)} %bitcast.103, (f32[4,4,128]{2,1,0:T(4,128)S(1)}, f32[4,4,128,128]{3,2,1,0:T(8,128)S(1)}) %tuple.133, (s32[]{:T(128)}, f32[8,4,4,128,128]{4,3,2,1,0:T(8,128)}, f32[4,4,128]{2,1,0:T(4,128)S(1)}, f32[4,4,128]{2,1,0:T(4,128)S(1)}, ...), branch_computations={%region_10.10_spmd, %region_11.12_spmd} | conditional | flops 68419600 | bytes 5161146 | solution.py:91
  391.4 6.1 %conditional.7 = ((f32[4,4,128]{2,1,0:T(4,128)S(1)}, f32[4,4,128,128]{3,2,1,0:T(8,128)S(1)})) conditional(s32[]{:T(128)} %bitcast.103, (f32[4,4,128]{2,1,0:T(4,128)S(1)}, f32[4,4,128,128]{3,2,1,0:T(8,128)S(1)}) %tuple.133, (s32[]{:T(128)}, f32[8,4,4,128,128]{4,3,2,1,0:T(8,128)}, f32[4,4,128]{2,1,0:T(4,128)S(1)}, f32[4,4,128]{2,1,0:T(4,128)S(1)}, ...), branch_computations={%region_10.10_spmd, %region_11.12_spmd} | conditional | flops 68419600 | bytes 5161146 | solution.py:91
  399.6 35.6 %collective-permute-start.4 = (bf16[2,128,2048]{2,1,0:T(8,128)(2,1)}, bf16[2,128,2048]{2,1,0:T(8,128)(2,1)S(1)}, u32[]{:S(2)}, u32[]{:S(2)}) collective-permute-start(bf16[2,128,2048]{2,1,0:T(8,128)(2,1)} %get-tuple-element.515), channel_id=1, source_target_pairs={{0,1},{1,0},{2,3},{3,2},{4,5},{5,4},{6,7},{7,6},{8,9},{9,8},{10,11... | collective-permute-start | bytes 3145736 | tf_op jit(solution)/shard_map/ppermute | solution.py:22
  (358 shorter events, 214.5 us)
Async XLA Ops:
  7.2 104.1 %copy-start = (bf16[1,256,4096]{2,1,0:T(8,128)(2,1)S(1)}, bf16[1,256,4096]{2,1,0:T(8,128)(2,1)}, u32[]{:S(2)}) copy-start(bf16[1,256,4096]{2,1,0:T(8,128)(2,1)} %param.18) | copy-start | bytes 6291460
  7.2 104.1 %all-gather.2.cloned.1.call-start = ((), (), s32[]{:S(2)}) async-start(), calls=%async_computation | async-start | bytes 8454144 | tf_op jit(solution)/shard_map/all_gather | solution.py:110
  17.4 104.3 %copy-start.4 = (s32[1,256]{1,0:T(1,128)S(1)}, s32[1,256]{1,0:T(1,128)}, u32[]{:S(2)}) copy-start(s32[1,256]{1,0:T(1,128)} %param.23) | copy-start | bytes 3076
  117.0 13.7 %copy-start.3 = (s32[1,256,7]{1,0,2:T(1,128)S(1)}, s32[1,256,7]{1,0,2:T(1,128)}, u32[]{:S(2)}) copy-start(s32[1,256,7]{1,0,2:T(1,128)} %param.22) | copy-start | bytes 21508
  117.0 13.9 %copy-start.5 = (s32[1,64]{1,0:T(1,128)S(1)}, s32[1,64]{1,0:T(1,128)}, u32[]{:S(2)}) copy-start(s32[1,64]{1,0:T(1,128)} %param.21) | copy-start | bytes 772
  117.3 5.1 %collective-permute-start.1 = (bf16[2,128,1024]{1,2,0:T(8,128)(2,1)S(1)}, bf16[2,128,1024]{1,2,0:T(8,128)(2,1)S(1)}, u32[]{:S(2)}, u32[]{:S(2)}) collective-permute-start(bf16[2,128,1024]{1,2,0:T(8,128)(2,1)S(1)} %copy.44), channel_id=1, source_target_pairs={{0,1},{1,0},{2,3},{3,2},{4,5},{5,4},{6,7},{7,6},{8,9},{9,8},{10,11... | collective-permute-start | bytes 1572872 | tf_op jit(solution)/shard_map/ppermute | solution.py:22
  119.5 11.8 %collective-permute-start = (bf16[2,128,2048]{2,1,0:T(8,128)(2,1)}, bf16[2,128,2048]{2,1,0:T(8,128)(2,1)}, u32[]{:S(2)}, u32[]{:S(2)}) collective-permute-start(bf16[2,128,2048]{2,1,0:T(8,128)(2,1)} %bitcast.110), channel_id=1, source_target_pairs={{0,1},{1,0},{2,3},{3,2},{4,5},{5,4},{6,7},{7,6},{8,9},{9,8},{10,11... | collective-permute-start | bytes 3145736 | tf_op jit(solution)/shard_map/ppermute | solution.py:22
  123.6 48.2 %collective-permute-start.2 = (bf16[4,128,1024]{1,2,0:T(8,128)(2,1)}, bf16[4,128,1024]{1,2,0:T(8,128)(2,1)}, u32[]{:S(2)}, u32[]{:S(2)}) collective-permute-start(bf16[4,128,1024]{1,2,0:T(8,128)(2,1)} %maximum_select_fusion), channel_id=1, source_target_pairs={{0,4},{1,5},{2,6},{3,7},{4,8},{5,9},{6,10},{7,11},{8,12},{9,13},{1... | collective-permute-start | bytes 3145736 | tf_op jit(solution)/shard_map/ppermute | solution.py:28
  126.5 70.8 %collective-permute-start.3 = (bf16[4,128,1024]{1,2,0:T(8,128)(2,1)}, bf16[4,128,1024]{1,2,0:T(8,128)(2,1)}, u32[]{:S(2)}, u32[]{:S(2)}) collective-permute-start(bf16[4,128,1024]{1,2,0:T(8,128)(2,1)} %maximum_select_fusion), channel_id=1, source_target_pairs={{0,2},{1,3},{2,4},{3,5},{4,6},{5,7},{6,8},{7,9},{8,10},{9,11},{10,... | collective-permute-start | bytes 3145736 | tf_op jit(solution)/shard_map/ppermute | solution.py:28
  265.7 54.0 %copy-start.1 = (f32[2,16,128]{2,1,0:T(8,128)S(1)}, f32[2,16,128]{2,1,0:T(8,128)}, u32[]{:S(2)}) copy-start(f32[2,16,128]{2,1,0:T(8,128)} %get-tuple-element.1001) | copy-start | bytes 49156 | tf_op jit(solution)/shard_map/while
  319.7 2.0 copy-start.2
  368.0 29.5 %copy-start.1 = (f32[2,16,128]{2,1,0:T(8,128)S(1)}, f32[2,16,128]{2,1,0:T(8,128)}, u32[]{:S(2)}) copy-start(f32[2,16,128]{2,1,0:T(8,128)} %get-tuple-element.1001) | copy-start | bytes 49156 | tf_op jit(solution)/shard_map/while
  397.6 2.0 copy-start.2
  399.6 38.1 %collective-permute-start.4 = (bf16[2,128,2048]{2,1,0:T(8,128)(2,1)}, bf16[2,128,2048]{2,1,0:T(8,128)(2,1)S(1)}, u32[]{:S(2)}, u32[]{:S(2)}) collective-permute-start(bf16[2,128,2048]{2,1,0:T(8,128)(2,1)} %get-tuple-element.515), channel_id=1, source_target_pairs={{0,1},{1,0},{2,3},{3,2},{4,5},{5,4},{6,7},{7,6},{8,9},{9,8},{10,11... | collective-permute-start | bytes 3145736 | tf_op jit(solution)/shard_map/ppermute | solution.py:22
Sparse Core Ops, SparseCore 0:
  17.5 93.7 all-gather.1
where the time goes:
time: 455 us; the launch traced here: 451 us
  waiting for transfers between devices  154 us (34%)
  local copies, waits for them, and re-layouts  99.6 us (22%)
  matrix products  48.2 us (11%)
  starting transfers between devices  46.4 us (10%)
  loops' own time  41.3 us (9%)
  other arithmetic  37.1 us (8%)
  between operations  14.2 us (3%)
  blocking collectives  10.1 us (2%)
    all_gather x1, waiting for transfers between devices, body(): lax.all_gather(columns, 'ctx', axis=0, tiled=True)  93.9 us
    ppermute x2, waiting for transfers between devices, passed_along(): return lax.ppermute(array, axis, pairs)  59.5 us
    ppermute x3, starting transfers between devices, from_partner(): return lax.ppermute(block, axis, route)  39.9 us
    dot_general x10, matrix products, compute(): jnp.einsum('ikgd,lkd->kgil', heads, keys, preferred_element_type=jnp.floa...  23.9 us
    while x12, local copies, waits for them, and re-layouts  20.5 us
    squeeze x20, local copies, waits for them, and re-layouts, fetch(): return lax.dynamic_index_in_dim(buffer, local, 0, keepdims=False)  19.4 us
    reduce_sum x10, other arithmetic, add(): total = total + jnp.sum(weights, axis=-1)  18.7 us
    dot_general x10, matrix products, add(): jnp.einsum('kgil,lkd->kgid', weights.astype(jnp.bfloat16), values, prefer...  18.5 us
  transfers between devices with their start and end apart: 6, of which 4 were waited for; matrix products, arithmetic and copies ran while one was open for 3% of the time, Pallas kernels for 0%

commit v1 on v0

v1 whole, which is shorter than its diff:
```python
import functools
import math

import jax
import jax.numpy as jnp
from jax import lax
from jax.experimental import pallas as pl
from jax.experimental.pallas import tpu as pltpu
from jax.sharding import PartitionSpec as P

HD = 128
QH = 16
KVH = 4
BLK = 128
MAXDOC = 8
GROUP = QH // KVH
CHIP_BLOCKS = 4
BACK = MAXDOC - 1
WINDOW = BACK + CHIP_BLOCKS
NEAR = BACK - CHIP_BLOCKS
HALF = QH * HD // 2
KW = KVH * HD // 2
SCALE2 = math.log2(math.e) / math.sqrt(HD)
LN2 = math.log(2.0)
MESH = pl.DeviceIdType.MESH
BF16 = jnp.bfloat16
F32 = jnp.float32
NT = (((1,), (1,)), ((), ()))


def kernel(
    n,
    tok_in,
    q_in,
    w_in,
    docs_ref,
    mask_ref,
    plan_ref,
    out_ref,
    stats_ref,
    tok,
    wbuf,
    q,
    kbuf,
    vbuf,
    prod,
    o,
    acc_s,
    m_s,
    l_s,
    lse_t,
    lse_b,
    picked,
    bias,
    loc_sem,
    tok_sem,
    q_sem,
    wx_send,
    wx_recv,
    s1_send,
    s1_recv,
    s2_send,
    s2_recv,
    kv_send,
    kv_recv,
    out_send,
    out_recv,
    st_send,
    st_recv,
):
    x = lax.axis_index("dp")
    ctx = lax.axis_index("ctx")
    chips = n * n
    core = lax.rem(ctx, 2)
    chip = lax.div(ctx, 2)
    z = lax.rem(chip, n)
    y = lax.div(chip, n)
    other = 1 - core
    partner = chip * 2 + other
    on_y = core == 0
    first_pos = jnp.where(on_y, y, z)
    ring_pos = jnp.where(on_y, z, y)

    def first_peer(step):
        pos = lax.rem(first_pos + step, n)
        return jnp.where(on_y, pos * n + z, y * n + pos) * 2 + core

    def ring_peer(step):
        pos = lax.rem(ring_pos + step, n)
        return jnp.where(on_y, y * n + pos, pos * n + z) * 2 + core

    after = lax.rem(chip + 1, chips) * 2 + core
    before = lax.rem(chip + chips - 1, chips) * 2 + core

    local = [
        pltpu.make_async_copy(tok_in.at[0], tok.at[pl.ds(core * 256, 256)], loc_sem.at[0]),
        pltpu.make_async_copy(
            q_in.at[0, :, pl.ds(pl.multiple_of(core * HALF, HALF), HALF)],
            q.at[pl.ds(core * 256, 256)],
            loc_sem.at[1],
        ),
    ]
    for copy in local:
        copy.start()

    barrier = pltpu.get_barrier_semaphore()
    peers = [(x, partner)]
    for step in range(1, 4):
        other_x = lax.rem(x + step, 4)
        peers += [(other_x, ctx), (other_x, partner)]
    peers += [(x, first_peer(step)) for step in range(1, n)]
    peers += [(x, ring_peer(1)), (x, ring_peer(n - 1)), (x, after), (x, before)]
    for peer in peers:
        pl.semaphore_signal(barrier, inc=1, device_id=peer, device_id_type=MESH)
    pl.semaphore_wait(barrier, len(peers))

    def remote(src, dst, send, recv, device):
        return pltpu.make_async_remote_copy(
            src_ref=src, dst_ref=dst, send_sem=send, recv_sem=recv, device_id=device, device_id_type=MESH
        )

    dest_core = lax.rem(x, 2)
    part = lax.div(x, 2)
    dest_a = jnp.where(dest_core == 0, z, y)
    dest_b = jnp.where(dest_core == 0, y, z)
    slot = wbuf.at[
        dest_a,
        dest_b,
        pl.ds(pl.multiple_of(core * 32, 32), 32),
        pl.ds(pl.multiple_of(part * KW, KW), KW),
    ]
    place = part * 2 + core
    dest_ctx = chip * 2 + dest_core
    piece_sends = [
        remote(w_in, slot, wx_send.at[step], wx_recv.at[place], (lax.rem(x + step, 4), dest_ctx))
        for step in range(1, 4)
    ]
    for copy in piece_sends:
        copy.start()
    piece_over = remote(w_in, slot, wx_send.at[0], wx_recv.at[place], (x, partner))

    @pl.when(dest_core == core)
    def _():
        pltpu.make_async_copy(w_in, slot, wx_recv.at[place]).start()

    @pl.when(dest_core != core)
    def _():
        piece_over.start()

    tok_send = remote(
        tok_in.at[0], tok.at[pl.ds(core * 256, 256)], tok_sem.at[0], tok_sem.at[1], (x, partner)
    )
    q_send = remote(
        q_in.at[0, :, pl.ds(pl.multiple_of(other * HALF, HALF), HALF)],
        q.at[pl.ds(core * 256, 256)],
        q_sem.at[0],
        q_sem.at[1],
        (x, partner),
    )
    mine = wbuf.at[ring_pos, first_pos]
    for k in range(4):
        quarter = wbuf.at[ring_pos, first_pos, pl.ds((k % 2) * 32, 32), pl.ds((k // 2) * KW, KW)]
        pltpu.make_async_copy(quarter, quarter, wx_recv.at[k]).wait()
    first_sends = [
        remote(mine, mine, s1_send.at[step], s1_recv.at[step], (x, first_peer(step)))
        for step in range(1, n)
    ]
    for copy in first_sends:
        copy.start()
    tok_send.start()
    q_send.start()

    base = chip * CHIP_BLOCKS - BACK

    def count(j, state):
        end = state[0] + docs_ref[0, j]
        return (end,) + tuple(
            state[1 + b] + jnp.where(base + b >= end, 1, 0) for b in range(WINDOW)
        )

    zero = jnp.int32(0)
    document = lax.fori_loop(0, docs_ref.shape[1], count, (zero,) * (WINDOW + 1))[1:]
    for i in range(CHIP_BLOCKS):
        for s in range(BACK):
            key = i + s
            keep = jnp.logical_and(document[key] == document[i + BACK], base + key >= 0)
            keep = jnp.logical_and(keep, mask_ref[BACK - s - 1, chip * CHIP_BLOCKS + i] == 1)
            bias[i * MAXDOC + s] = jnp.where(keep, jnp.float32(0.0), jnp.float32(-jnp.inf))

    for step in range(1, n):
        source = lax.rem(first_pos + n - step, n)
        got = wbuf.at[ring_pos, source]
        pltpu.make_async_copy(got, got, s1_recv.at[step]).wait()

    half = n // 2
    steps = n // 2

    def ring_copy(way, k, h):
        shift = n - (k - 1) if way == 0 else k - 1
        chunk = wbuf.at[lax.rem(ring_pos + shift, n), pl.ds(h * half, half)]
        to = ring_peer(1) if way == 0 else ring_peer(n - 1)
        return remote(chunk, chunk, s2_send.at[way, k, h], s2_recv.at[way, k, h], (x, to))

    def ring_got(way, k, h):
        shift = n - k if way == 0 else k
        chunk = wbuf.at[lax.rem(ring_pos + shift, n), pl.ds(h * half, half)]
        pltpu.make_async_copy(chunk, chunk, s2_recv.at[way, k, h]).wait()

    ring_sends = []

    def ring_start(way, k, h):
        if k < steps or h == way:
            copy = ring_copy(way, k, h)
            copy.start()
            ring_sends.append(copy)

    order = ((0, 0), (1, 1), (0, 1), (1, 0))
    for k in range(1, steps + 1):
        for way, h in order:
            if k > 1:
                ring_got(way, k - 1, h)
            ring_start(way, k, h)
    ring_got(0, steps, 0)
    ring_got(1, steps, 1)

    for copy in local:
        copy.wait()
    tok_send.wait_recv()
    q_send.wait_recv()

    def project(column, dest):
        prod[...] = jnp.zeros_like(prod)

        @pl.loop(0, n)
        def _(k):
            rows = [
                wbuf[
                    jnp.where(on_y, j, k),
                    jnp.where(on_y, k, j),
                    :,
                    pl.ds(column, KW),
                ]
                for j in range(n)
            ]
            taken = tok[:, pl.ds(pl.multiple_of(k * (64 * n), 64 * n), 64 * n)]
            prod[...] += jnp.dot(taken, jnp.concatenate(rows, axis=0), preferred_element_type=F32)

        dest[pl.ds(BACK * BLK, CHIP_BLOCKS * BLK), :] = prod[...].astype(BF16)

    kv_sends = []

    def pass_on(index, buf, src, dst, count):
        copy = remote(
            buf.at[pl.ds(src * BLK, count * BLK)],
            buf.at[pl.ds(dst * BLK, count * BLK)],
            kv_send.at[index],
            kv_recv.at[index],
            (x, after),
        )
        copy.start()
        kv_sends.append(copy)

    project(0, kbuf)
    pass_on(0, kbuf, BACK, NEAR, CHIP_BLOCKS)
    project(KW, vbuf)
    pass_on(1, vbuf, BACK, NEAR, CHIP_BLOCKS)
    kv_sends[0].wait_recv()
    pass_on(2, kbuf, NEAR + 1, 0, NEAR)
    kv_sends[1].wait_recv()
    pass_on(3, vbuf, NEAR + 1, 0, NEAR)

    causal = (
        lax.broadcasted_iota(jnp.int32, (GROUP * BLK, BLK), 1)
        <= lax.broadcasted_iota(jnp.int32, (GROUP * BLK, BLK), 0) % BLK
    )
    lane = lax.broadcasted_iota(jnp.int32, (BLK, BLK), 1)

    def scores(i, g, low, high):
        rows = q[pl.ds(i * BLK, BLK), pl.ds(pl.multiple_of(g * (GROUP * HD), GROUP * HD), GROUP * HD)]
        heads = jnp.concatenate([rows[:, h * HD : (h + 1) * HD] for h in range(GROUP)], axis=0)
        columns = pl.ds(pl.multiple_of(g * HD, HD), HD)
        keys = kbuf[pl.ds(low * BLK, (high - low) * BLK), columns]
        table = lax.dot_general(heads, keys, NT, preferred_element_type=F32)
        tiles = []
        for key in range(low, high):
            tile = table[:, (key - low) * BLK : (key - low + 1) * BLK] * SCALE2
            if key == i + BACK:
                tile = jnp.where(causal, tile, -jnp.inf)
            else:
                tile = tile + bias[i * MAXDOC + key - i]
            tiles.append(tile)
        return tiles

    def weigh(tiles, top, g, low, high):
        weights = [jnp.exp2(tile - top) for tile in tiles]
        total = functools.reduce(jnp.add, weights)
        total = jnp.sum(total, axis=1, keepdims=True)
        columns = pl.ds(pl.multiple_of(g * HD, HD), HD)
        values = vbuf[pl.ds(low * BLK, (high - low) * BLK), columns]
        packed = jnp.concatenate([w.astype(BF16) for w in weights], axis=1)
        return total, jnp.dot(packed, values, preferred_element_type=F32)

    def finish(i, g, top, total, summed):
        result = (summed / total).astype(BF16)
        lse = (top + jnp.log2(total)) * LN2
        for h in range(GROUP):
            column = pl.multiple_of(g * (GROUP * HD) + h * HD, HD)
            o[pl.ds(i * BLK, BLK), pl.ds(column, HD)] = result[h * BLK : (h + 1) * BLK]
            lse_t[i] = jnp.where(lane == g * GROUP + h, lse[h * BLK : (h + 1) * BLK], lse_t[i])

    def highest(tiles):
        return jnp.max(functools.reduce(jnp.maximum, tiles), axis=1, keepdims=True)

    lse_t[...] = jnp.zeros_like(lse_t)

    def near_part(i):
        @pl.loop(0, KVH // 2)
        def _(g):
            low, high = NEAR, i + BACK + 1
            tiles = scores(i, g, low, high)
            top = highest(tiles)
            total, summed = weigh(tiles, top, g, low, high)
            if i == CHIP_BLOCKS - 1:
                finish(i, g, top, total, summed)
            else:
                acc_s[i, g] = summed
                m_s[i, g] = top
                l_s[i, g] = total

    def far_part(i):
        @pl.loop(0, KVH // 2)
        def _(g):
            low, high = i, NEAR
            tiles = scores(i, g, low, high)
            top = jnp.maximum(highest(tiles), m_s[i, g])
            keep = jnp.exp2(m_s[i, g] - top)
            total, summed = weigh(tiles, top, g, low, high)
            finish(i, g, top, total + l_s[i, g] * keep, summed + acc_s[i, g] * keep)

    def out_copy(i):
        rows = pl.ds((i % 2) * BLK, BLK)
        columns = pl.ds(pl.multiple_of(core * HALF, HALF), HALF)
        return o.at[pl.ds(i * BLK, BLK)], out_ref.at[0, rows, columns]

    def hand_out(i):
        lse_b[i] = lse_t[i].T[: QH // 2]
        src, dst = out_copy(i)

        @pl.when(core == i // 2)
        def _():
            pltpu.make_async_copy(src, dst, loc_sem.at[2 + i]).start()

        @pl.when(core != i // 2)
        def _():
            remote(src, dst, out_send.at[i % 2], out_recv.at[i % 2], (x, partner)).start()

    for i in range(CHIP_BLOCKS - 1, -1, -1):
        near_part(i)
    hand_out(CHIP_BLOCKS - 1)
    kv_sends[2].wait_recv()
    kv_sends[3].wait_recv()
    for i in (2, 0, 1):
        far_part(i)
        hand_out(i)

    for t in range(2):
        for j in range(2):
            slot_id = chip * CHIP_BLOCKS + t * 2 + j
            chosen = jnp.zeros((QH // 2, BLK), F32)
            for i in range(CHIP_BLOCKS):
                here = plan_ref[0, chip * CHIP_BLOCKS + i] == slot_id
                chosen += jnp.where(here, jnp.float32(1.0), jnp.float32(0.0)) * lse_b[i]
            picked[t, :, pl.ds(j * BLK, BLK)] = chosen
    stat_rows = stats_ref.at[0, pl.ds(pl.multiple_of(core * (QH // 2), QH // 2), QH // 2)]
    keep_stats = pltpu.make_async_copy(picked.at[core], stat_rows, loc_sem.at[6])
    give_stats = remote(picked.at[other], stat_rows, st_send, st_recv, (x, partner))
    keep_stats.start()
    give_stats.start()

    for i in range(CHIP_BLOCKS):
        src, dst = out_copy(i)

        @pl.when(core == i // 2)
        def _():
            pltpu.make_async_copy(src, dst, loc_sem.at[2 + i]).wait()

        @pl.when(core != i // 2)
        def _():
            copy = remote(src, dst, out_send.at[i % 2], out_recv.at[i % 2], (x, partner))
            copy.wait_send()
            copy.wait_recv()

    keep_stats.wait()
    give_stats.wait_send()
    give_stats.wait_recv()
    for copy in piece_sends + first_sends + ring_sends + kv_sends:
        copy.wait_send()
    tok_send.wait_send()
    q_send.wait_send()

    @pl.when(dest_core != core)
    def _():
        piece_over.wait_send()


def body(n, tokens, queries, kv_weight, doc_blocks, block_mask, plan):
    wide = 64 * n * n
    smem = pl.BlockSpec(memory_space=pltpu.SMEM)
    hbm = pl.BlockSpec(memory_space=pl.ANY)
    dma = pltpu.SemaphoreType.DMA
    parts = KVH // 2
    rows = CHIP_BLOCKS * BLK
    early = CHIP_BLOCKS - 1
    return pl.pallas_call(
        functools.partial(kernel, n),
        out_shape=(
            jax.ShapeDtypeStruct(queries.shape, BF16),
            jax.ShapeDtypeStruct((1, QH, tokens.shape[1]), F32),
        ),
        in_specs=[hbm, hbm, hbm, smem, smem, smem],
        out_specs=(hbm, hbm),
        scratch_shapes=[
            pltpu.VMEM((rows, wide), BF16),
            pltpu.VMEM((n, n, 64, 2 * KW), BF16),
            pltpu.VMEM((rows, HALF), BF16),
            pltpu.VMEM((WINDOW * BLK, KW), BF16),
            pltpu.VMEM((WINDOW * BLK, KW), BF16),
            pltpu.VMEM((rows, KW), F32),
            pltpu.VMEM((rows, HALF), BF16),
            pltpu.VMEM((early, parts, GROUP * BLK, HD), F32),
            pltpu.VMEM((early, parts, GROUP * BLK, 1), F32),
            pltpu.VMEM((early, parts, GROUP * BLK, 1), F32),
            pltpu.VMEM((CHIP_BLOCKS, BLK, BLK), F32),
            pltpu.VMEM((CHIP_BLOCKS, QH // 2, BLK), F32),
            pltpu.VMEM((2, QH // 2, 2 * BLK), F32),
            pltpu.SMEM((CHIP_BLOCKS * MAXDOC,), F32),
            dma((7,)),
            dma((2,)),
            dma((2,)),
            dma((4,)),
            dma((4,)),
            dma((n,)),
            dma((n,)),
            dma((2, n // 2 + 1, 2)),
            dma((2, n // 2 + 1, 2)),
            dma((4,)),
            dma((4,)),
            dma((2,)),
            dma((2,)),
            dma,
            dma,
        ],
        compiler_params=pltpu.CompilerParams(
            collective_id=0, has_side_effects=True, vmem_limit_bytes=50 * 1024 * 1024
        ),
    )(tokens, queries, kv_weight, doc_blocks, block_mask[0].T, plan)


def solution(mesh):
    in_specs = (
        P("dp", "ctx", None),
        P("dp", "ctx", None),
        P("ctx", "dp"),
        P("dp", None),
        P("dp", None, None),
        P("dp", None),
    )
    out_specs = (P("dp", "ctx", None), P("dp", None, "ctx"))
    n = math.isqrt(mesh.shape["ctx"] // 2)
    return jax.shard_map(
        functools.partial(body, n), mesh=mesh, in_specs=in_specs, out_specs=out_specs, check_vma=False
    )
```

time: 455 us -> 97.5 us (0.21)
  the two profiles are of different devices: /device:TPU:51 before, /device:TPU:1 now
where the time goes in v1:
time: 97.5 us; the launch traced here: 97.2 us
  Pallas kernels  91 us (93%)
  local copies, waits for them, and re-layouts  5.55 us (6%)
    pallas_call x1, Pallas kernels, body(): pl.pallas_call(functools.partial(kernel, n), out_shape=(jax.ShapeDtypeStr...  91 us
    unnamed x11, local copies, waits for them, and re-layouts  5.55 us

profile of v1, /device:TPU:1, one launch (start us, length us, event | category | flops | bytes accessed | tf_op | source)
XLA Modules:
  0.0 97.2 jit_solution(16641535751261544639)
XLA Ops:
  0.6 0.7 copy.10
  1.3 0.0 copy-start
  1.3 1.2 %copy-done = bf16[1,256,2048]{2,1,0:T(8,128)(2,1)S(1)} copy-done((bf16[1,256,2048]{2,1,0:T(8,128)(2,1)S(1)}, bf16[1,256,2048]{2,1,0:T(8,128)(2,1)}, u32[]{:S(2)}) %copy-start) | copy-done | bytes 1048600
  2.6 0.0 copy-start.1
  2.6 0.7 copy-done.1
  3.3 0.0 copy-start.2
  3.3 0.7 copy-done.2
  3.9 0.0 copy-start.3
  4.0 0.7 copy-done.3
  4.6 91.0 %shard_map.77 = (bf16[1,256,2048]{2,1,0:T(8,128)(2,1)S(1)}, f32[1,16,256]{2,1,0:T(8,128)S(1)}) custom-call(bf16[1,256,4096]{2,1,0:T(8,128)(2,1)} %tok_in.1, bf16[1,256,2048]{2,1,0:T(8,128)(2,1)S(1)} %copy-done, bf16[32,256]{1,0:T(8,128)(2,1)S(1)} %copy-done.1, s32[1,64]{1,0:T(1,128)S(1)} %copy-done.3, s32[7,256]{1,0:T(8,128)S(1)} %bitcast.5, ...), custom_call_target="tpu_custom_call" | custom-call | tf_op jit(solution)/shard_map/pallas_call | solution.py:414
  95.6 1.0 %copy.13 = bf16[1,256,2048]{2,1,0:T(8,128)(2,1)} copy(bf16[1,256,2048]{2,1,0:T(8,128)(2,1)S(1)} %get-tuple-element.4) | data formatting | bytes 2097152
  96.6 0.6 copy.14
Async XLA Ops:
  1.3 1.2 %copy-start = (bf16[1,256,2048]{2,1,0:T(8,128)(2,1)S(1)}, bf16[1,256,2048]{2,1,0:T(8,128)(2,1)}, u32[]{:S(2)}) copy-start(bf16[1,256,2048]{2,1,0:T(8,128)(2,1)} %q_in.1) | copy-start | bytes 3145732
  2.6 0.7 copy-start.1
  3.3 0.7 copy-start.2
  3.9 0.7 copy-start.3

commit v2 on v1

v2 whole, which is shorter than its diff:
```python
import functools
import math

import jax
import jax.numpy as jnp
from jax import lax
from jax.experimental import pallas as pl
from jax.experimental.pallas import tpu as pltpu
from jax.sharding import PartitionSpec as P

HD = 128
QH = 16
KVH = 4
BLK = 128
MAXDOC = 8
GROUP = QH // KVH
CHIP_BLOCKS = 4
BACK = MAXDOC - 1
WINDOW = BACK + CHIP_BLOCKS
NEAR = BACK - CHIP_BLOCKS
HALF = QH * HD // 2
KW = KVH * HD // 2
SCALE2 = math.log2(math.e) / math.sqrt(HD)
LN2 = math.log(2.0)
MESH = pl.DeviceIdType.MESH
BF16 = jnp.bfloat16
F32 = jnp.float32
NT = (((1,), (1,)), ((), ()))


def kernel(
    n,
    tok_in,
    q_in,
    w_in,
    docs_in,
    mask_in,
    plan_in,
    out_ref,
    stats_ref,
    tok,
    wbuf,
    q,
    kv,
    prod,
    o,
    acc_s,
    m_s,
    l_s,
    lse_b,
    picked,
    docs,
    mask,
    plan,
    bias,
    loc_sem,
    tok_sem,
    q_sem,
    wx_send,
    wx_recv,
    s1_send,
    s1_recv,
    s2_send,
    s2_recv,
    kv_send,
    kv_recv,
    out_loc,
    out_send,
    out_recv,
    st_send,
    st_recv,
):
    x = lax.axis_index("dp")
    ctx = lax.axis_index("ctx")
    chips = n * n
    half = n // 2
    core = lax.rem(ctx, 2)
    chip = lax.div(ctx, 2)
    z = lax.rem(chip, n)
    y = lax.div(chip, n)
    other = 1 - core
    partner = chip * 2 + other
    on_y = core == 0
    first_pos = jnp.where(on_y, y, z)
    ring_pos = jnp.where(on_y, z, y)

    def first_peer(step):
        pos = lax.rem(first_pos + step, n)
        return jnp.where(on_y, pos * n + z, y * n + pos) * 2 + core

    def ring_peer(step):
        pos = lax.rem(ring_pos + step, n)
        return jnp.where(on_y, y * n + pos, pos * n + z) * 2 + core

    after = lax.rem(chip + 1, chips) * 2 + core
    before = lax.rem(chip + chips - 1, chips) * 2 + core

    def remote(src, dst, send, recv, device):
        return pltpu.make_async_remote_copy(
            src_ref=src, dst_ref=dst, send_sem=send, recv_sem=recv, device_id=device, device_id_type=MESH
        )

    def arrived(ref, sem):
        pltpu.make_async_copy(ref, ref, sem).wait()

    barrier = pltpu.get_barrier_semaphore()
    peers = [(x, partner)]
    for step in range(1, 4):
        other_x = lax.rem(x + step, 4)
        peers += [(other_x, ctx), (other_x, partner)]
    peers += [(x, first_peer(step)) for step in range(1, n)]
    peers += [(x, ring_peer(1)), (x, ring_peer(n - 1)), (x, after), (x, before)]
    for peer in peers:
        pl.semaphore_signal(barrier, inc=1, device_id=peer, device_id_type=MESH)

    local = [
        pltpu.make_async_copy(tok_in.at[0], tok.at[pl.ds(core * 256, 256)], loc_sem.at[0]),
        pltpu.make_async_copy(
            q_in.at[0, :, pl.ds(pl.multiple_of(core * HALF, HALF), HALF)],
            q.at[pl.ds(core * 256, 256)],
            loc_sem.at[1],
        ),
    ]
    tables = [
        pltpu.make_async_copy(docs_in, docs, loc_sem.at[2]),
        pltpu.make_async_copy(mask_in, mask, loc_sem.at[3]),
        pltpu.make_async_copy(plan_in, plan, loc_sem.at[4]),
    ]
    for copy in local + tables:
        copy.start()
    pl.semaphore_wait(barrier, len(peers))

    dest_core = lax.rem(x, 2)
    part = lax.div(x, 2)
    dest_a = jnp.where(dest_core == 0, z, y)
    dest_b = jnp.where(dest_core == 0, y, z)
    slot = wbuf.at[
        dest_a,
        dest_b,
        pl.ds(pl.multiple_of(core * 32, 32), 32),
        pl.ds(pl.multiple_of(part * KW, KW), KW),
    ]
    place = part * 2 + core
    dest_ctx = chip * 2 + dest_core
    piece_sends = [
        remote(w_in, slot, wx_send.at[step], wx_recv.at[place], (lax.rem(x + step, 4), dest_ctx))
        for step in (2, 1, 3)
    ]
    for copy in piece_sends:
        copy.start()
    piece_over = remote(w_in, slot, wx_send.at[0], wx_recv.at[place], (x, partner))

    @pl.when(dest_core == core)
    def _():
        pltpu.make_async_copy(w_in, slot, wx_recv.at[place]).start()

    @pl.when(dest_core != core)
    def _():
        piece_over.start()

    tok_send = remote(
        tok_in.at[0], tok.at[pl.ds(core * 256, 256)], tok_sem.at[0], tok_sem.at[1], (x, partner)
    )
    q_send = remote(
        q_in.at[0, :, pl.ds(pl.multiple_of(other * HALF, HALF), HALF)],
        q.at[pl.ds(core * 256, 256)],
        q_sem.at[0],
        q_sem.at[1],
        (x, partner),
    )
    for k in range(4):
        arrived(
            wbuf.at[ring_pos, first_pos, pl.ds((k % 2) * 32, 32), pl.ds((k // 2) * KW, KW)],
            wx_recv.at[k],
        )

    steps = half

    def ring_copy(way, k, h):
        row = n - (k - 1) if way == 0 else k - 1
        chunk = wbuf.at[lax.rem(ring_pos + row, n), pl.ds(h * half, half)]
        to = ring_peer(1) if way == 0 else ring_peer(n - 1)
        return remote(chunk, chunk, s2_send.at[way, k, h], s2_recv.at[way, k, h], (x, to))

    def ring_got(way, k, h):
        row = n - k if way == 0 else k
        arrived(wbuf.at[lax.rem(ring_pos + row, n), pl.ds(h * half, half)], s2_recv.at[way, k, h])

    sends = []

    def start(copy):
        copy.start()
        sends.append(copy)

    def ring_start(way, k, h):
        if k < steps or h == way:
            start(ring_copy(way, k, h))

    def pair_operands(m):
        taken, rows = [], []
        for j in range(n):
            row = 2 * m + j // half
            pair = 2 * (j % half)
            rows.append(wbuf[jnp.where(on_y, 2 * m, row), jnp.where(on_y, j, pair)])
            rows.append(wbuf[jnp.where(on_y, 2 * m + 1, row), jnp.where(on_y, j, pair + 1)])
            column = jnp.where(on_y, j * n + 2 * m, row * n + pair) * 64
            taken.append(tok[:, pl.ds(pl.multiple_of(column, 128), 128)])
        rows = jnp.concatenate(rows, axis=0)
        return jnp.concatenate(taken, axis=1), rows

    def head_columns(rows, g):
        return jnp.concatenate(
            [rows[:, g * HD : (g + 1) * HD], rows[:, KW + g * HD : KW + (g + 1) * HD]], axis=1
        )

    def project(m, fresh):
        taken, rows = pair_operands(m)
        for g in range(KVH // 2):
            part_sum = jnp.dot(taken, head_columns(rows, g), preferred_element_type=F32)
            prod[g] = part_sum if fresh else prod[g] + part_sum

    pairs = half
    even = lax.rem(ring_pos, 2) == 0
    middle = lax.div(ring_pos, 2)
    near_side = jnp.where(even, pairs - 1, 1)
    far_side = jnp.where(even, 1, pairs - 1)
    units = {
        2: [middle],
        4: [middle, lax.rem(middle + 1, pairs)],
        8: [
            middle,
            lax.rem(middle + near_side, pairs),
            lax.rem(middle + far_side, pairs),
            lax.rem(middle + 2, pairs),
        ],
    }[n]

    mine = wbuf.at[ring_pos, first_pos]
    for step in sorted(range(1, n), key=lambda step: min(step, n - step), reverse=True):
        start(remote(mine, mine, s1_send.at[step], s1_recv.at[step], (x, first_peer(step))))
    tok_send.start()
    q_send.start()

    for copy in tables:
        copy.wait()
    base = chip * CHIP_BLOCKS - BACK

    def count(j, state):
        end = state[0] + docs[0, j]
        return (end,) + tuple(
            state[1 + b] + jnp.where(base + b >= end, 1, 0) for b in range(WINDOW)
        )

    zero = jnp.int32(0)
    document = lax.fori_loop(0, docs.shape[1], count, (zero,) * (WINDOW + 1))[1:]
    for i in range(CHIP_BLOCKS):
        for s in range(BACK):
            key = i + s
            keep = jnp.logical_and(document[key] == document[i + BACK], base + key >= 0)
            gate = mask[BACK - s - 1, 0, chip * CHIP_BLOCKS + i] == 1
            keep = jnp.logical_and(keep, gate)
            bias[i * MAXDOC + s] = jnp.where(
                keep, jnp.float32(0.0), jnp.float32(-jnp.inf)
            )

    for step in range(1, n):
        source = lax.rem(first_pos + n - step, n)
        arrived(wbuf.at[ring_pos, source], s1_recv.at[step])

    order = ((0, 0), (1, 1), (0, 1), (1, 0))
    for k in range(1, steps + 1):
        for way, h in order:
            if k > 1:
                ring_got(way, k - 1, h)
            ring_start(way, k, h)
    ring_got(0, steps, 0)
    ring_got(1, steps, 1)
    local[0].wait()
    tok_send.wait_recv()
    for unit in range(steps - 1):
        project(units[unit], unit == 0)

    def passed(stage, g):
        if stage == 0:
            src, dst, count = BACK, NEAR, CHIP_BLOCKS
        else:
            src, dst, count = NEAR + 1, 0, NEAR
        return remote(
            kv.at[g, pl.ds(src, count)],
            kv.at[g, pl.ds(dst, count)],
            kv_send.at[stage, g],
            kv_recv.at[stage, g],
            (x, after),
        )

    taken, rows = pair_operands(units[-1])
    for g in range(KVH // 2):
        pair_kv = jnp.dot(taken, head_columns(rows, g), preferred_element_type=F32)
        if pairs > 1:
            pair_kv += prod[g]
        pair_kv = pair_kv.astype(BF16)
        for i in range(CHIP_BLOCKS):
            block = pair_kv[i * BLK : (i + 1) * BLK]
            kv[g, BACK + i, 0] = block[:, :HD]
            kv[g, BACK + i, 1] = block[:, HD:].T
        passed(0, g).start()

    local[1].wait()
    q_send.wait_recv()

    causal = (
        lax.broadcasted_iota(jnp.int32, (BLK, GROUP * BLK), 0)
        <= lax.broadcasted_iota(jnp.int32, (BLK, GROUP * BLK), 1) % BLK
    )

    def attend(i, g, low, high, own, old):
        rows = q[
            pl.ds(pl.multiple_of(i * BLK, BLK), BLK),
            pl.ds(pl.multiple_of(g * (GROUP * HD), GROUP * HD), GROUP * HD),
        ]
        heads = jnp.concatenate([rows[:, h * HD : (h + 1) * HD] for h in range(GROUP)], axis=0)
        tiles, offsets = [], []
        top = old
        for key in range(low, high):
            tile = lax.dot_general(kv[g, key, 0], heads, NT, preferred_element_type=F32)
            if own and key == high - 1:
                tile = jnp.where(causal, tile, -jnp.inf)
                offset = None
                highest = jnp.max(tile, axis=0, keepdims=True) * SCALE2
            else:
                offset = bias[i * BACK + key]
                highest = jnp.max(tile, axis=0, keepdims=True) * SCALE2 + offset
            tiles.append(tile)
            offsets.append(offset)
            top = highest if top is None else jnp.maximum(top, highest)
        total = None
        packed = []
        for tile, offset in zip(tiles, offsets):
            level = top if offset is None else top - offset
            weights = jnp.exp2(tile * SCALE2 - level)
            packed.append(weights.astype(BF16))
            amount = jnp.sum(weights, axis=0, keepdims=True)
            total = amount if total is None else total + amount
        values = jnp.concatenate([kv[g, key, 1] for key in range(low, high)], axis=1)
        summed = jnp.dot(values, jnp.concatenate(packed, axis=0), preferred_element_type=F32)
        return top, total, summed

    def join(i, g, low, high):
        old = m_s[i, g]
        top, total, summed = attend(i, g, low, high, False, old)
        keep = jnp.exp2(old - top)
        return top, total + l_s[i, g] * keep, summed + acc_s[i, g] * keep

    def finish(i, g, top, total, summed):
        result = (summed * (1.0 / total)).astype(BF16)
        lse = (top + jnp.log2(total)) * LN2
        for h in range(GROUP):
            o[g, i, :, h * HD : (h + 1) * HD] = result[:, h * BLK : (h + 1) * BLK].T
            lse_b[i, pl.ds(g * GROUP + h, 1), :] = lse[:, h * BLK : (h + 1) * BLK]

    def out_copy(i, g):
        rows = pl.ds((i % 2) * BLK, BLK)
        there = pl.ds(pl.multiple_of(core * HALF + g * (GROUP * HD), GROUP * HD), GROUP * HD)
        return o.at[g, i], out_ref.at[0, rows, there]

    def hand_out(i, g):
        src, dst = out_copy(i, g)

        @pl.when(core == i // 2)
        def _():
            pltpu.make_async_copy(src, dst, out_loc.at[i % 2, g]).start()

        @pl.when(core != i // 2)
        def _():
            remote(src, dst, out_send.at[i % 2, g], out_recv.at[i % 2, g], (x, partner)).start()

    last = CHIP_BLOCKS - 1

    for g in range(KVH // 2):
        for i in range(CHIP_BLOCKS):
            top, total, summed = attend(i, g, BACK, BACK + i + 1, True, None)
            acc_s[i, g] = summed
            m_s[i, g] = top
            l_s[i, g] = total

    for g in range(KVH // 2):
        passed(0, g).wait_recv()
        passed(1, g).start()

        @pl.loop(0, CHIP_BLOCKS)
        def _(i, g=g):
            top, total, summed = join(i, g, NEAR, BACK)
            acc_s[i, g] = summed
            m_s[i, g] = top
            l_s[i, g] = total

        finish(last, g, m_s[last, g], l_s[last, g], acc_s[last, g])
        hand_out(last, g)

    for g in range(KVH // 2):
        passed(1, g).wait_recv()
        for i in (2, 1, 0):
            finish(i, g, *join(i, g, i, NEAR))
            hand_out(i, g)

    for t in range(2):
        for j in range(2):
            slot_id = chip * CHIP_BLOCKS + t * 2 + j
            chosen = jnp.zeros((QH // 2, BLK), F32)
            for i in range(CHIP_BLOCKS):
                here = plan[0, chip * CHIP_BLOCKS + i] == slot_id
                chosen += jnp.where(here, jnp.float32(1.0), jnp.float32(0.0)) * lse_b[i]
            picked[t, :, pl.ds(j * BLK, BLK)] = chosen
    stat_rows = stats_ref.at[0, pl.ds(pl.multiple_of(core * (QH // 2), QH // 2), QH // 2)]
    keep_stats = pltpu.make_async_copy(picked.at[core], stat_rows, loc_sem.at[5])
    give_stats = remote(picked.at[other], stat_rows, st_send, st_recv, (x, partner))
    give_stats.start()
    keep_stats.start()

    for copy in piece_sends + sends:
        copy.wait_send()
    tok_send.wait_send()
    q_send.wait_send()

    @pl.when(dest_core != core)
    def _():
        piece_over.wait_send()

    for stage in range(2):
        for g in range(KVH // 2):
            passed(stage, g).wait_send()

    for i in range(CHIP_BLOCKS):
        for g in range(KVH // 2):
            src, dst = out_copy(i, g)

            @pl.when(core == i // 2)
            def _():
                pltpu.make_async_copy(src, dst, out_loc.at[i % 2, g]).wait()

            @pl.when(core != i // 2)
            def _():
                copy = remote(src, dst, out_send.at[i % 2, g], out_recv.at[i % 2, g], (x, partner))
                copy.wait_send()
                copy.wait_recv()

    keep_stats.wait()
    give_stats.wait_send()
    give_stats.wait_recv()


def body(n, tokens, queries, kv_weight, doc_blocks, block_mask, plan):
    wide = 64 * n * n
    hbm = pl.BlockSpec(memory_space=pltpu.HBM)
    dma = pltpu.SemaphoreType.DMA
    parts = KVH // 2
    rows = CHIP_BLOCKS * BLK
    gates = jnp.transpose(block_mask, (2, 0, 1))
    return pl.pallas_call(
        functools.partial(kernel, n),
        out_shape=(
            jax.ShapeDtypeStruct(queries.shape, BF16),
            jax.ShapeDtypeStruct((1, QH, tokens.shape[1]), F32),
        ),
        in_specs=[hbm] * 6,
        out_specs=(hbm, hbm),
        scratch_shapes=[
            pltpu.VMEM((rows, wide), BF16),
            pltpu.VMEM((n, n, 64, 2 * KW), BF16),
            pltpu.VMEM((rows, HALF), BF16),
            pltpu.VMEM((parts, WINDOW, 2, BLK, HD), BF16),
            pltpu.VMEM((parts, rows, 2 * HD), F32),
            pltpu.VMEM((parts, CHIP_BLOCKS, BLK, GROUP * HD), BF16),
            pltpu.VMEM((CHIP_BLOCKS, parts, HD, GROUP * BLK), F32),
            pltpu.VMEM((CHIP_BLOCKS, parts, 1, GROUP * BLK), F32),
            pltpu.VMEM((CHIP_BLOCKS, parts, 1, GROUP * BLK), F32),
            pltpu.VMEM((CHIP_BLOCKS, QH // 2, BLK), F32),
            pltpu.VMEM((2, QH // 2, 2 * BLK), F32),
            pltpu.SMEM(doc_blocks.shape, jnp.int32),
            pltpu.SMEM(gates.shape, jnp.int32),
            pltpu.SMEM(plan.shape, jnp.int32),
            pltpu.SMEM((CHIP_BLOCKS * MAXDOC,), F32),
            dma((6,)),
            dma((2,)),
            dma((2,)),
            dma((4,)),
            dma((4,)),
            dma((n,)),
            dma((n,)),
            dma((2, n // 2 + 1, 2)),
            dma((2, n // 2 + 1, 2)),
            dma((2, parts)),
            dma((2, parts)),
            dma((2, parts)),
            dma((2, parts)),
            dma((2, parts)),
            dma,
            dma,
        ],
        compiler_params=pltpu.CompilerParams(
            collective_id=0, has_side_effects=True, vmem_limit_bytes=60 * 1024 * 1024
        ),
    )(tokens, queries, kv_weight, doc_blocks, gates, plan)


def solution(mesh):
    in_specs = (
        P("dp", "ctx", None),
        P("dp", "ctx", None),
        P("ctx", "dp"),
        P("dp", None),
        P("dp", None, None),
        P("dp", None),
    )
    out_specs = (P("dp", "ctx", None), P("dp", None, "ctx"))
    n = math.isqrt(mesh.shape["ctx"] // 2)
    return jax.shard_map(
        functools.partial(body, n), mesh=mesh, in_specs=in_specs, out_specs=out_specs, check_vma=False
    )
```

time: 97.5 us -> 82.7 us (0.85)
  Pallas kernels: 91 us -> 78.9 us
  local copies, waits for them, and re-layouts: 5.55 us -> 2.92 us
    pallas_call x1, Pallas kernels: 91 us -> 78.9 us  [body(): pl.pallas_call(functools.partial(kernel, n), out_shape=(jax.ShapeDtypeStr...]
    unnamed x11 -> x4, local copies, waits for them, and re-layouts: 5.55 us -> 2.92 us
where the time goes in v2:
time: 82.7 us; the launch traced here: 82.5 us
  Pallas kernels  78.9 us (95%)
  local copies, waits for them, and re-layouts  2.92 us (4%)
    pallas_call x1, Pallas kernels, body(): pl.pallas_call(functools.partial(kernel, n), out_shape=(jax.ShapeDtypeStr...  78.9 us
    unnamed x4, local copies, waits for them, and re-layouts  2.92 us

profile of v2, /device:TPU:1, one launch (start us, length us, event | category | flops | bytes accessed | tf_op | source)
XLA Modules:
  0.0 82.5 jit_solution(422305271131560358)
XLA Ops:
  0.6 78.9 %shard_map.77 = (bf16[1,256,2048]{2,1,0:T(8,128)(2,1)}, f32[1,16,256]{2,1,0:T(8,128)}) custom-call(bf16[1,256,4096]{2,1,0:T(8,128)(2,1)} %tok_in.1, bf16[1,256,2048]{2,1,0:T(8,128)(2,1)} %q_in.1, bf16[32,256]{1,0:T(8,128)(2,1)} %w_in.1, s32[1,64]{1,0:T(1,128)} %docs_in.1, s32[7,1,256]{2,1,0:T(1,128)} %bitcast.1, s32[1,256]{1,0:T(1,128)} %plan_in.1), custom_call_target="tpu_custom_call" | custom-call | tf_op jit(solution)/shard_map/pallas_call | solution.py:459
  79.5 0.0 copy-start
  79.5 2.3 %copy.10 = bf16[1,256,2048]{2,1,0:T(8,128)(2,1)} copy(bf16[1,256,2048]{2,1,0:T(8,128)(2,1)} %get-tuple-element.4) | data formatting | bytes 2097152
  81.9 0.0 copy-done
  81.9 0.6 copy.11
Async XLA Ops:
  79.5 2.3 %copy-start = (f32[1,16,256]{2,1,0:T(8,128)S(1)}, f32[1,16,256]{2,1,0:T(8,128)}, u32[]{:S(2)}) copy-start(f32[1,16,256]{2,1,0:T(8,128)} %get-tuple-element.5) | copy-start | bytes 49156

commit v3 on v2

--- a/solution.py
+++ b/solution.py
@@ -80,17 +80,20 @@
     y = lax.div(chip, n)
     other = 1 - core
     partner = chip * 2 + other
-    on_y = core == 0
-    first_pos = jnp.where(on_y, y, z)
-    ring_pos = jnp.where(on_y, z, y)
+
+    def by_core(zero, one):
+        return zero + core * (one - zero)
+
+    first_pos = by_core(y, z)
+    ring_pos = by_core(z, y)
 
     def first_peer(step):
         pos = lax.rem(first_pos + step, n)
-        return jnp.where(on_y, pos * n + z, y * n + pos) * 2 + core
+        return by_core(pos * n + z, y * n + pos) * 2 + core
 
     def ring_peer(step):
         pos = lax.rem(ring_pos + step, n)
-        return jnp.where(on_y, y * n + pos, pos * n + z) * 2 + core
+        return by_core(y * n + pos, pos * n + z) * 2 + core
 
     after = lax.rem(chip + 1, chips) * 2 + core
     before = lax.rem(chip + chips - 1, chips) * 2 + core
@@ -126,14 +129,12 @@
         pltpu.make_async_copy(mask_in, mask, loc_sem.at[3]),
         pltpu.make_async_copy(plan_in, plan, loc_sem.at[4]),
     ]
-    for copy in local + tables:
-        copy.start()
     pl.semaphore_wait(barrier, len(peers))
 
     dest_core = lax.rem(x, 2)
     part = lax.div(x, 2)
-    dest_a = jnp.where(dest_core == 0, z, y)
-    dest_b = jnp.where(dest_core == 0, y, z)
+    dest_a = z + dest_core * (y - z)
+    dest_b = y + dest_core * (z - y)
     slot = wbuf.at[
         dest_a,
         dest_b,
@@ -158,6 +159,9 @@
     def _():
         piece_over.start()
 
+    for copy in tables + local:
+        copy.start()
+
     tok_send = remote(
         tok_in.at[0], tok.at[pl.ds(core * 256, 256)], tok_sem.at[0], tok_sem.at[1], (x, partner)
     )
@@ -201,9 +205,9 @@
         for j in range(n):
             row = 2 * m + j // half
             pair = 2 * (j % half)
-            rows.append(wbuf[jnp.where(on_y, 2 * m, row), jnp.where(on_y, j, pair)])
-            rows.append(wbuf[jnp.where(on_y, 2 * m + 1, row), jnp.where(on_y, j, pair + 1)])
-            column = jnp.where(on_y, j * n + 2 * m, row * n + pair) * 64
+            rows.append(wbuf[by_core(2 * m, row), by_core(j, pair)])
+            rows.append(wbuf[by_core(2 * m + 1, row), by_core(j, pair + 1)])
+            column = by_core(j * n + 2 * m, row * n + pair) * 64
             taken.append(tok[:, pl.ds(pl.multiple_of(column, 128), 128)])
         rows = jnp.concatenate(rows, axis=0)
         return jnp.concatenate(taken, axis=1), rows
@@ -220,12 +224,11 @@
             prod[g] = part_sum if fresh else prod[g] + part_sum
 
     pairs = half
-    even = lax.rem(ring_pos, 2) == 0
+    odd = lax.rem(ring_pos, 2)
     middle = lax.div(ring_pos, 2)
-    near_side = jnp.where(even, pairs - 1, 1)
-    far_side = jnp.where(even, 1, pairs - 1)
+    near_side = (pairs - 1) - odd * (pairs - 2)
+    far_side = 1 + odd * (pairs - 2)
     units = {
-        2: [middle],
         4: [middle, lax.rem(middle + 1, pairs)],
         8: [
             middle,
@@ -236,7 +239,7 @@
     }[n]
 
     mine = wbuf.at[ring_pos, first_pos]
-    for step in sorted(range(1, n), key=lambda step: min(step, n - step), reverse=True):
+    for step in sorted(range(1, n), key=lambda step: -min(step, n - step)):
         start(remote(mine, mine, s1_send.at[step], s1_recv.at[step], (x, first_peer(step))))
     tok_send.start()
     q_send.start()
@@ -273,13 +276,13 @@
             if k > 1:
                 ring_got(way, k - 1, h)
             ring_start(way, k, h)
+        if k > 1:
+            if k == 2:
+                local[0].wait()
+                tok_send.wait_recv()
+            project(units[k - 2], k == 2)
     ring_got(0, steps, 0)
     ring_got(1, steps, 1)
-    local[0].wait()
-    tok_send.wait_recv()
-    for unit in range(steps - 1):
-        project(units[unit], unit == 0)
-
     def passed(stage, g):
         if stage == 0:
             src, dst, count = BACK, NEAR, CHIP_BLOCKS

time: 82.7 us -> 81 us (0.979)
  Pallas kernels: 78.9 us -> 77.3 us
    pallas_call x1, Pallas kernels: 78.9 us -> 77.3 us  [body(): pl.pallas_call(functools.partial(kernel, n), out_shape=(jax.ShapeDtypeStr...]
where the time goes in v3:
time: 81 us; the launch traced here: 80.8 us
  Pallas kernels  77.3 us (95%)
  local copies, waits for them, and re-layouts  2.92 us (4%)
    pallas_call x1, Pallas kernels, body(): pl.pallas_call(functools.partial(kernel, n), out_shape=(jax.ShapeDtypeStr...  77.3 us
    unnamed x4, local copies, waits for them, and re-layouts  2.92 us

profile of v3, /device:TPU:1, one launch (start us, length us, event | category | flops | bytes accessed | tf_op | source)
XLA Modules:
  0.0 80.8 jit_solution(14501658963641449355)
XLA Ops:
  0.6 77.3 %shard_map.77 = (bf16[1,256,2048]{2,1,0:T(8,128)(2,1)}, f32[1,16,256]{2,1,0:T(8,128)}) custom-call(bf16[1,256,4096]{2,1,0:T(8,128)(2,1)} %tok_in.1, bf16[1,256,2048]{2,1,0:T(8,128)(2,1)} %q_in.1, bf16[32,256]{1,0:T(8,128)(2,1)} %w_in.1, s32[1,64]{1,0:T(1,128)} %docs_in.1, s32[7,1,256]{2,1,0:T(1,128)} %bitcast.1, s32[1,256]{1,0:T(1,128)} %plan_in.1), custom_call_target="tpu_custom_call" | custom-call | tf_op jit(solution)/shard_map/pallas_call | solution.py:462
  77.9 0.0 copy-start
  77.9 2.3 %copy.10 = bf16[1,256,2048]{2,1,0:T(8,128)(2,1)} copy(bf16[1,256,2048]{2,1,0:T(8,128)(2,1)} %get-tuple-element.4) | data formatting | bytes 2097152
  80.2 0.0 copy-done
  80.2 0.6 copy.11
Async XLA Ops:
  77.9 2.3 %copy-start = (f32[1,16,256]{2,1,0:T(8,128)S(1)}, f32[1,16,256]{2,1,0:T(8,128)}, u32[]{:S(2)}) copy-start(f32[1,16,256]{2,1,0:T(8,128)} %get-tuple-element.5) | copy-start | bytes 49156
